TPU v7x, 32 devices: a whole 2x2x4 slice. The times are simulated.
32 devices in a mesh: row: 8 (over z, x), col: 4 (over y, core).
Axes of the slice: x: 2, y: 2, z: 4, core: 2. Of those that a mesh axis runs over, the one named last changes fastest.
Arguments:
- positions: float32 [3, 8192], P(None, ('row', 'col')), may hold values from -6 to 6
- features: bfloat16 [128, 8192], P(None, ('row', 'col')), may hold values from -6 to 6
- fill: int32 [64], P(('row', 'col')), may hold values from 64 to 128, as said below
- tiles: int32 [256, 2], P(('row', 'col')), may hold values from 0 to 15, as said below
- tile_count: int32 [32], P(('row', 'col')), may hold values from 2 to 8, as said below
- w_radial: float32 [64, 32], replicated, may hold values from -1 to 1
- w_left: bfloat16 [128, 64], replicated, may hold values from -0.5 to 0.5
- w_right: bfloat16 [128, 64], replicated, may hold values from -0.5 to 0.5
- w_hidden: bfloat16 [64, 64], replicated, may hold values from -0.75 to 0.75
- w_out: bfloat16 [64], replicated, may hold values from -0.25 to 0.25
Outputs:
- forces: float32 [3, 8192], P(None, ('row', 'col'))
- bead_energy: float32 [8192], P(('row', 'col'))
Inputs may be any that keep to these rules, and one draw needn't show every extreme that they name: `fill`: at least 64; some cluster holds 128. `tiles`: A device's 8 slots name distinct cluster pairs; the first entry is below 8, the second below 16; some device has the pair of the last clusters of both groups. `tile_count`: at least 2; some device has all 8 slots live.
All inputs are finite; a program needn't handle non-finite values.
Results may differ from a plain program's by a relative error of at most 0.0045.
Values may be sent and summed in bfloat16 or wider, within the bound.
A program may use at most 64 MiB of HBM per device.

v0:
```python
import functools
import math

import jax
import jax.numpy as jnp
from jax import lax
from jax.experimental import pallas as pl
from jax.experimental.pallas import tpu as pltpu
from jax.sharding import PartitionSpec as P

CL = 128
SOFT = 0.01
RANGE = 6.0
GROUP = 8
STEP = 16
PICK = 16
MESH = pl.DeviceIdType.MESH
F32 = jnp.float32
BF16 = jnp.bfloat16


def peers(nrow, ncol, i, j):
    along_col = [(d, lax.rem(j + d, ncol)) for d in range(1, ncol)]
    along_row = [(d, lax.rem(i + d, nrow)) for d in range(1, nrow)]
    return along_col, along_row


def enter(i, j, along_col, along_row):
    barrier = pltpu.get_barrier_semaphore()
    for _, c in along_col:
        pl.semaphore_signal(barrier, inc=1, device_id=(i, c), device_id_type=MESH)
    for _, r in along_row:
        pl.semaphore_signal(barrier, inc=1, device_id=(r, j), device_id_type=MESH)
    return barrier, len(along_col) + len(along_row)


def gather_kernel(
    nrow, ncol, inner, pos_ref, feat_ref, fill_ref, wl_ref, wr_ref,
    rowc_ref, rowp_ref, colc_ref, colp_ref, send_sem, recv_sem,
):
    i = lax.axis_index("row")
    j = lax.axis_index("col")
    outer = nrow // inner
    at_out = i // inner
    at_in = i % inner
    cols = [lax.rem(j + d, ncol) for d in range(1, ncol)]
    outs = [lax.rem(at_out + d, outer) * inner + at_in for d in range(1, outer)]
    origins = [lax.rem(at_out + outer - d, outer) * inner + at_in for d in range(1, outer)]
    mates = [at_out * inner + lax.rem(at_in + d, inner) for d in range(1, inner)]
    barrier = pltpu.get_barrier_semaphore()
    for target in [(r, j) for r in outs + mates] + [(i, c) for c in cols]:
        pl.semaphore_signal(barrier, inc=1, device_id=target, device_id_type=MESH)
    beads = pos_ref.shape[1]
    lane = lax.broadcasted_iota(jnp.int32, (1, CL), 1)
    live = jnp.concatenate(
        [(lane < fill_ref[k]).astype(F32) for k in range(beads // CL)], 1
    )
    coords = jnp.concatenate([pos_ref[...], live], 0)
    rowc_ref[j] = coords
    colc_ref[i] = coords
    dims = (((1,), (0,)), ((), ()))
    feats = feat_ref[...]
    rowp_ref[j] = lax.dot_general(wl_ref[...], feats, dims, preferred_element_type=F32).astype(BF16)
    colp_ref[i] = lax.dot_general(wr_ref[...], feats, dims, preferred_element_type=F32).astype(BF16)
    pl.semaphore_wait(barrier, len(outs) + len(mates) + len(cols))
    started = []

    def send(refs, slot, target):
        copies = []
        for ref in refs:
            k = len(started)
            copy = pltpu.make_async_remote_copy(
                src_ref=ref.at[slot], dst_ref=ref.at[slot],
                send_sem=send_sem.at[k], recv_sem=recv_sem.at[k],
                device_id=target, device_id_type=MESH,
            )
            copy.start()
            started.append(copy)
            copies.append(copy)
        return copies

    late = []
    hops = [send((colp_ref, colc_ref), i, (r, j)) for r in outs]
    for r in mates:
        late += send((colp_ref, colc_ref), i, (r, j))
    for c in cols:
        late += send((rowp_ref, rowc_ref), j, (i, c))
    for copies, origin in zip(hops, origins):
        for copy in copies:
            copy.wait_recv()
        for r in mates:
            late += send((colp_ref, colc_ref), origin, (r, j))
    for copies in hops:
        for copy in copies:
            copy.wait_send()
    for copy in late:
        copy.wait()


def scatter_kernel(
    nrow, ncol, first_ref, second_ref, force_ref, energy_ref, row_in, col_in, send_sem, recv_sem
):
    i = lax.axis_index("row")
    j = lax.axis_index("col")
    along_col, along_row = peers(nrow, ncol, i, j)
    barrier, count = enter(i, j, along_col, along_row)
    pl.semaphore_wait(barrier, count)
    started = []
    for d, r in along_row:
        started.append((second_ref.at[r], col_in.at[d], (r, j)))
    for d, c in along_col:
        started.append((first_ref.at[c], row_in.at[d], (i, c)))
    copies = []
    for k, (src, dst, target) in enumerate(started):
        copy = pltpu.make_async_remote_copy(
            src_ref=src, dst_ref=dst, send_sem=send_sem.at[k], recv_sem=recv_sem.at[k],
            device_id=target, device_id_type=MESH,
        )
        copy.start()
        copies.append(copy)
    total = first_ref[j]
    other = second_ref[i]
    for copy in copies:
        copy.wait()
    for d in range(1, ncol):
        total = total + row_in[d]
    for d in range(1, nrow):
        other = other + col_in[d]
    force_ref[...] = total[:3] + other[:3]
    energy_ref[...] = total[3:4]


def tile_kernel(
    cpd, ncol, tiles_ref, count_ref, rowc_ref, rowp_ref, colc_ref, colp_ref,
    wrad_ref, whid_ref, wout_ref, first_ref, second_ref,
    acc_ref, dist_ref, phi_ref, slope_ref, proj_ref, pair_ref, base_ref, wout_ref8, pick_ref,
):
    row = lax.axis_index("row")
    col = lax.axis_index("col")
    nbasis, hidden = wrad_ref.shape
    clusters = acc_ref.shape[0]
    spacing = RANGE / (nbasis - 1)
    scale = math.sqrt(math.log2(math.e))
    back = -2.0 / (spacing * scale)
    live_count = count_ref[0]
    acc_ref[...] = jnp.zeros_like(acc_ref)
    second_ref[...] = jnp.zeros_like(second_ref)

    wide = jnp.concatenate(
        [0.5 * wrad_ref[...].T, jnp.zeros((hidden, CL - nbasis), F32)], 1
    )
    base_ref[...] = wide
    whid = whid_ref[...] * jnp.asarray(0.5, BF16)
    wout = jnp.broadcast_to(wout_ref[...].astype(F32), (8, hidden)).T
    wout_ref8[...] = jnp.broadcast_to(wout[:, 0:1], (hidden, CL))
    centers = lax.broadcasted_iota(jnp.int32, (nbasis, CL), 0).astype(F32) * scale
    lanes64 = lax.broadcasted_iota(jnp.int32, (hidden, CL), 1)
    lanes = lax.broadcasted_iota(jnp.int32, (CL, CL), 1)
    ident = (lax.broadcasted_iota(jnp.int32, (CL, CL), 0) == lanes).astype(F32)
    pick = lax.broadcasted_iota(jnp.int32, (PICK, 2 * CL), 0)
    side = lax.broadcasted_iota(jnp.int32, (PICK, 2 * CL), 1) < CL
    for a in range(STEP):
        pick_ref[a] = jnp.where(jnp.logical_and(pick == a, side), 1.0, 0.0).astype(BF16)

    one = jnp.asarray(1.0, BF16)

    @pl.loop(0, live_count)
    def _(slot):
        first = tiles_ref[0, slot]
        other = tiles_ref[1, slot]
        col_a = first // cpd
        row_b = other // cpd
        at_a = pl.ds(pl.multiple_of(first % cpd * CL, CL), CL)
        at_b = pl.ds(pl.multiple_of(other % cpd * CL, CL), CL)
        same = jnp.logical_and(
            jnp.logical_and(col_a == col, row_b == row), first % cpd == other % cpd
        ).astype(F32)
        left = rowc_ref[col_a, :, at_a]
        mine = jnp.concatenate([left, left], 0).T
        proj_ref[...] = 0.5 * rowp_ref[col_a, :, at_a].astype(F32)
        right = colc_ref[row_b, :, at_b]
        pair_ref[...] = 0.5 * colp_ref[row_b, :, at_b].astype(F32)
        beads = jnp.sum(left[3:4]).astype(jnp.int32)
        chunks = (beads + STEP - 1) // STEP
        dx = mine[:, 0:1] - right[0:1]
        dy = mine[:, 1:2] - right[1:2]
        dz = mine[:, 2:3] - right[2:3]
        dist = jnp.sqrt(dx * dx + dy * dy + dz * dz + SOFT)
        dist_ref[...] = dist * (scale / spacing)

        def step(start):
            rolled = pltpu.roll(proj_ref[...], lax.rem(nbasis - start + CL, CL), 1)
            lhs = jnp.where(lanes64 < nbasis, base_ref[...], rolled)[:, : nbasis + PICK].astype(BF16)
            for half in range(0, STEP, GROUP):
                rows = pl.ds(pl.multiple_of(start + half, GROUP), GROUP)
                scaled = dist_ref[rows, :]
                for a in range(GROUP):
                    off = scaled[a : a + 1] - centers
                    basis = jnp.exp2(-(off * off))
                    lift = basis * off
                    x1 = jnp.concatenate(
                        [jnp.concatenate([basis, lift], 1).astype(BF16), pick_ref[half + a]], 0
                    )
                    y1 = jnp.dot(lhs, x1, preferred_element_type=F32)
                    h = (y1[:, :CL] + pair_ref[...]).astype(BF16)
                    e = y1[:, CL:].astype(BF16)
                    t = jnp.tanh(h)
                    u = one + t
                    s = h * u
                    d = u + (one - t) * s
                    x2 = jnp.concatenate([s, d * e], 1)
                    y2 = jnp.dot(whid, x2, preferred_element_type=F32)
                    h = y2[:, :CL]
                    t = jnp.tanh(h)
                    u = (1.0 + t) * wout_ref8[...]
                    s = h * u
                    g = (u + (1.0 - t) * s) * y2[:, CL:]
                    spot = pl.ds(pl.multiple_of(start * 8, 8) + (half + a) * 8, 8)
                    phi_ref[spot, :] = jnp.sum(s.reshape(hidden // 8, 8, CL), 0)
                    slope_ref[spot, :] = jnp.sum(g.reshape(hidden // 8, 8, CL), 0)

        @pl.loop(0, chunks // 2)
        def _(c):
            start = pl.multiple_of(c * (2 * STEP), 2 * STEP)
            step(start)
            step(start + STEP)

        @pl.when(chunks % 2 == 1)
        def _():
            step(pl.multiple_of((chunks - 1) * STEP, STEP))

        dist = dist_ref[...] * (spacing / scale)
        slope = slope_ref[pl.ds(0, CL, stride=8), :]
        phi = phi_ref[pl.ds(0, CL, stride=8), :]
        for k in range(1, 8):
            slope = slope + slope_ref[pl.ds(k, CL, stride=8), :]
            phi = phi + phi_ref[pl.ds(k, CL, stride=8), :]
        both = jnp.logical_and(mine[:, 3:4] * right[3:4] > 0.5, same * ident < 0.5)
        weight = jnp.where(both, back * slope / dist, 0.0)
        phi = jnp.where(both, phi, 0.0)
        wx = weight * dx
        wy = weight * dy
        wz = weight * dz
        energy = jnp.sum(phi, 1, keepdims=True)
        fx = -jnp.sum(wx, 1, keepdims=True)
        fy = -jnp.sum(wy, 1, keepdims=True)
        fz = -jnp.sum(wz, 1, keepdims=True)
        acc_ref[first] = acc_ref[first] + jnp.where(
            lanes == 0, fx, jnp.where(lanes == 1, fy, jnp.where(lanes == 2, fz, energy))
        )
        for k, part in enumerate((wx, wy, wz)):
            total = jnp.sum(part, 0, keepdims=True)
            second_ref[row_b, k : k + 1, at_b] = second_ref[row_b, k : k + 1, at_b] + total

    for k in range(clusters):
        place = (k // cpd, slice(None), slice(k % cpd * CL, k % cpd * CL + CL))
        first_ref[place] = acc_ref[k][:, :8].T


def body(nrow, ncol, positions, features, fill, tiles, tile_count, w_radial, w_left, w_right, w_hidden, w_out):
    beads = positions.shape[1]
    hidden = w_radial.shape[0]
    cpd = fill.shape[0]
    vmem = pl.BlockSpec(memory_space=pltpu.VMEM)
    smem = pl.BlockSpec(memory_space=pltpu.SMEM)
    sends = nrow + ncol - 2
    inner = 2 if nrow % 2 == 0 else 1
    gathered = pl.pallas_call(
        functools.partial(gather_kernel, nrow, ncol, inner),
        name="gather",
        out_shape=(
            jax.ShapeDtypeStruct((ncol, 4, beads), F32),
            jax.ShapeDtypeStruct((ncol, hidden, beads), BF16),
            jax.ShapeDtypeStruct((nrow, 4, beads), F32),
            jax.ShapeDtypeStruct((nrow, hidden, beads), BF16),
        ),
        in_specs=[vmem, vmem, smem, vmem, vmem],
        out_specs=(vmem,) * 4,
        scratch_shapes=[
            pltpu.SemaphoreType.DMA((2 * sends,)),
            pltpu.SemaphoreType.DMA((2 * sends,)),
        ],
        compiler_params=pltpu.CompilerParams(collective_id=0, has_side_effects=True),
    )(positions, features, fill, w_left.T, w_right.T)
    firsts, seconds = pl.pallas_call(
        functools.partial(tile_kernel, cpd, ncol),
        name="tiles",
        out_shape=(
            jax.ShapeDtypeStruct((ncol, 8, beads), F32),
            jax.ShapeDtypeStruct((nrow, 8, beads), F32),
        ),
        in_specs=[smem, smem] + [vmem] * 7,
        out_specs=(vmem, vmem),
        scratch_shapes=[
            pltpu.VMEM((ncol * cpd, CL, CL), F32),
            pltpu.VMEM((CL, CL), F32),
            pltpu.VMEM((CL * 8, CL), F32),
            pltpu.VMEM((CL * 8, CL), F32),
            pltpu.VMEM((hidden, CL), F32),
            pltpu.VMEM((hidden, CL), F32),
            pltpu.VMEM((hidden, CL), F32),
            pltpu.VMEM((hidden, CL), F32),
            pltpu.VMEM((STEP, PICK, 2 * CL), BF16),
        ],
    )(tiles.T, tile_count, *gathered, w_radial.T, w_hidden, w_out[None, :])
    forces, energy = pl.pallas_call(
        functools.partial(scatter_kernel, nrow, ncol),
        name="scatter",
        out_shape=(
            jax.ShapeDtypeStruct((3, beads), F32),
            jax.ShapeDtypeStruct((1, beads), F32),
        ),
        in_specs=[vmem, vmem],
        out_specs=(vmem, vmem),
        scratch_shapes=[
            pltpu.VMEM((ncol, 8, beads), F32),
            pltpu.VMEM((nrow, 8, beads), F32),
            pltpu.SemaphoreType.DMA((sends,)),
            pltpu.SemaphoreType.DMA((sends,)),
        ],
        compiler_params=pltpu.CompilerParams(collective_id=1, has_side_effects=True),
    )(firsts, seconds)
    return forces, energy[0]


def solution(mesh):
    nrow, ncol = mesh.shape["row"], mesh.shape["col"]
    return jax.shard_map(
        functools.partial(body, nrow, ncol),
        mesh=mesh,
        in_specs=(
            P(None, ("row", "col")),
            P(None, ("row", "col")),
            P(("row", "col")),
            P(("row", "col"), None),
            P(("row", "col")),
            P(),
            P(),
            P(),
            P(),
            P(),
        ),
        out_specs=(P(None, ("row", "col")), P(("row", "col"))),
        check_vma=False,
    )
```

profile of v0, /device:TPU:0, one launch (start us, length us, event | category | flops | bytes accessed | tf_op | source)
XLA Modules:
  0.0 56.9 jit_solution(10862969015586725591)
XLA Ops:
  1.3 15.3 %gather.1 = (f32[4,4,256]{2,1,0:T(4,128)}, bf16[4,64,256]{2,1,0:T(8,128)(2,1)}, f32[8,4,256]{2,1,0:T(4,128)}, bf16[8,64,256]{2,1,0:T(8,128)(2,1)}) custom-call(f32[3,256]{1,0:T(4,128)} %pos_ref.1, bf16[128,256]{1,0:T(8,128)(2,1)} %feat_ref.1, s32[2]{0:T(128)} %fill_ref.1, bf16[64,128]{1,0:T(8,128)(2,1)} %bitcast.6, bf16[64,128]{1,0:T(8,128)(2,1)} %bitcast.7), custom_call_target="tpu_custom_call" | custom-call | tf_op jit(solution)/shard_map/gather/pallas_call | solution.py:268
  16.5 13.2 %tiles.1 = (f32[4,8,256]{2,1,0:T(8,128)}, f32[8,8,256]{2,1,0:T(8,128)}) custom-call(s32[2,8]{1,0:T(2,128)} %bitcast.9, s32[1]{0:T(128)S(6)} %copy.14.count_ref, f32[4,4,256]{2,1,0:T(4,128)} %get-tuple-element.10.rowc_ref, bf16[4,64,256]{2,1,0:T(8,128)(2,1)} %get-tuple-element.11.rowp_ref, f32[8,4,256]{2,1,0:T(4,128)} %get-tuple-element.12.colc_ref, ...), custom_call_target="tpu_custom_call" | custom-call | tf_op jit(solution)/shard_map/tiles/pallas_call | solution.py:285
  29.7 25.3 %scatter.1 = (f32[3,256]{1,0:T(4,128)}, f32[1,256]{1,0:T(1,128)}) custom-call(f32[4,8,256]{2,1,0:T(8,128)} %get-tuple-element.14.first_ref, f32[8,8,256]{2,1,0:T(8,128)} %get-tuple-element.15.second_ref), custom_call_target="tpu_custom_call" | custom-call | tf_op jit(solution)/shard_map/scatter/pallas_call | solution.py:306
  55.0 0.0 copy-start
  55.0 0.7 %copy-done = f32[3,256]{1,0:T(4,128)S(1)} copy-done((f32[3,256]{1,0:T(4,128)S(1)}, f32[3,256]{1,0:T(4,128)}, u32[]{:S(2)}) %copy-start) | copy-done | bytes 3096
  55.7 0.0 copy-start.1
  55.7 0.6 %copy.15 = f32[3,256]{1,0:T(4,128)} copy(f32[3,256]{1,0:T(4,128)S(1)} %copy-done) | data formatting | bytes 6144
  56.3 0.1 copy-done.1
  56.3 0.6 copy.16
Async XLA Ops:
  55.0 0.7 %copy-start = (f32[3,256]{1,0:T(4,128)S(1)}, f32[3,256]{1,0:T(4,128)}, u32[]{:S(2)}) copy-start(f32[3,256]{1,0:T(4,128)} %get-tuple-element.20) | copy-start | bytes 9220
  55.7 0.7 %copy-start.1 = (f32[1,256]{1,0:T(1,128)S(1)}, f32[1,256]{1,0:T(1,128)}, u32[]{:S(2)}) copy-start(f32[1,256]{1,0:T(1,128)} %get-tuple-element.17) | copy-start | bytes 3076
where the time goes:
time: 57.4 us; the launch traced here: 56.9 us
  Pallas kernels  53.7 us (94%)
  local copies, waits for them, and re-layouts  1.9 us (3%)
  between operations  1.3 us (2%)
    pallas_call x1, Pallas kernels, body(): pl.pallas_call(functools.partial(scatter_kernel, nrow, ncol), name='scatt...  25.3 us
    pallas_call x1, Pallas kernels, body(): pl.pallas_call(functools.partial(gather_kernel, nrow, ncol, inner), name=...  15.3 us
    pallas_call x1, Pallas kernels, body(): pl.pallas_call(functools.partial(tile_kernel, cpd, ncol), name='tiles', o...  13.2 us
    unnamed x6, local copies, waits for them, and re-layouts  1.9 us

commit v1 on v0

--- a/solution.py
+++ b/solution.py
@@ -14,6 +14,9 @@
 GROUP = 8
 STEP = 16
 PICK = 16
+SEG = 16
+PAIR = 16
+WIDTHS = (5, 6, 7, 8)
 MESH = pl.DeviceIdType.MESH
 F32 = jnp.float32
 BF16 = jnp.bfloat16
@@ -133,7 +136,8 @@
 def tile_kernel(
     cpd, ncol, tiles_ref, count_ref, rowc_ref, rowp_ref, colc_ref, colp_ref,
     wrad_ref, whid_ref, wout_ref, first_ref, second_ref,
-    acc_ref, dist_ref, phi_ref, slope_ref, proj_ref, pair_ref, base_ref, wout_ref8, pick_ref,
+    acc_ref, dist_ref, pack_ref, phi_ref, slope_ref, nphi_ref, nslope_ref,
+    proj_ref, pair_src, pair_ref, base_ref, wout_ref8, cent_ref, pick_ref,
 ):
     row = lax.axis_index("row")
     col = lax.axis_index("col")
@@ -146,23 +150,35 @@
     acc_ref[...] = jnp.zeros_like(acc_ref)
     second_ref[...] = jnp.zeros_like(second_ref)
 
-    wide = jnp.concatenate(
-        [0.5 * wrad_ref[...].T, jnp.zeros((hidden, CL - nbasis), F32)], 1
+    depth = 2 * nbasis + PICK
+    wide = 0.5 * wrad_ref[...].T
+    coarse = wide.astype(BF16).astype(F32)
+    base_ref[...] = jnp.concatenate(
+        [coarse, jnp.zeros((hidden, PICK), F32), wide - coarse,
+         jnp.zeros((hidden, CL - depth), F32)], 1
     )
-    base_ref[...] = wide
     whid = whid_ref[...] * jnp.asarray(0.5, BF16)
     wout = jnp.broadcast_to(wout_ref[...].astype(F32), (8, hidden)).T
     wout_ref8[...] = jnp.broadcast_to(wout[:, 0:1], (hidden, CL))
-    centers = lax.broadcasted_iota(jnp.int32, (nbasis, CL), 0).astype(F32) * scale
+    cent_ref[...] = lax.broadcasted_iota(jnp.int32, (nbasis, CL), 0).astype(F32) * scale
     lanes64 = lax.broadcasted_iota(jnp.int32, (hidden, CL), 1)
+    inside = jnp.logical_and(lanes64 >= nbasis, lanes64 < nbasis + PICK)
+    segs64 = lanes64 // SEG
+    segs = lax.broadcasted_iota(jnp.int32, (CL // 8, CL), 1) // SEG
     lanes = lax.broadcasted_iota(jnp.int32, (CL, CL), 1)
     ident = (lax.broadcasted_iota(jnp.int32, (CL, CL), 0) == lanes).astype(F32)
     pick = lax.broadcasted_iota(jnp.int32, (PICK, 2 * CL), 0)
-    side = lax.broadcasted_iota(jnp.int32, (PICK, 2 * CL), 1) < CL
-    for a in range(STEP):
-        pick_ref[a] = jnp.where(jnp.logical_and(pick == a, side), 1.0, 0.0).astype(BF16)
-
-    one = jnp.asarray(1.0, BF16)
+    pick_lane = lax.broadcasted_iota(jnp.int32, (PICK, 2 * CL), 1)
+    for used in WIDTHS:
+        for a in range(STEP):
+            if a % 8 < used:
+                source = jnp.where(pick_lane < used * SEG, a % 8, pick_lane // SEG) + a // 8 * 8
+                hit = jnp.logical_and(pick == source, pick_lane < CL)
+                pick_ref[used - WIDTHS[0], a] = jnp.where(hit, 1.0, 0.0).astype(BF16)
+
+    def shift(value, amount):
+        amount = amount % CL
+        return pltpu.roll(value, amount, 1) if amount else value
 
     @pl.loop(0, live_count)
     def _(slot):
@@ -179,62 +195,106 @@
         mine = jnp.concatenate([left, left], 0).T
         proj_ref[...] = 0.5 * rowp_ref[col_a, :, at_a].astype(F32)
         right = colc_ref[row_b, :, at_b]
-        pair_ref[...] = 0.5 * colp_ref[row_b, :, at_b].astype(F32)
+        pair_src[...] = 0.5 * colp_ref[row_b, :, at_b].astype(F32)
         beads = jnp.sum(left[3:4]).astype(jnp.int32)
         chunks = (beads + STEP - 1) // STEP
+        across = jnp.sum(right[3:4]).astype(jnp.int32)
+        width = jnp.maximum((across + SEG - 1) // SEG, WIDTHS[0])
         dx = mine[:, 0:1] - right[0:1]
         dy = mine[:, 1:2] - right[1:2]
         dz = mine[:, 2:3] - right[2:3]
         dist = jnp.sqrt(dx * dx + dy * dy + dz * dz + SOFT)
         dist_ref[...] = dist * (scale / spacing)
 
-        def step(start):
+        def enter(start, used, lhs, half, a):
+            scaled = pack_ref[pl.ds(start + (half + a), 1), :]
+            off = scaled - cent_ref[...]
+            basis = jnp.exp2(-(off * off))
+            lift = basis * off
+            bump = jnp.concatenate([basis, lift], 1).astype(BF16)
+            x1 = jnp.concatenate([bump, pick_ref[used - WIDTHS[0], half + a], bump], 0)
+            y1 = jnp.dot(lhs, x1, preferred_element_type=F32)
+            h = y1[:, :CL] + pair_ref[a if used < 8 else 0]
+            t = jnp.tanh(h)
+            u = 1.0 + t
+            s = h * u
+            d = (u + (1.0 - t) * s) * y1[:, CL:]
+            return jnp.concatenate([s, d], 1).astype(BF16)
+
+        def leave(start, half, a, y2):
+            h = y2[:, :CL]
+            t = jnp.tanh(h)
+            u = (1.0 + t) * wout_ref8[...]
+            s = h * u
+            g = (u + (1.0 - t) * s) * y2[:, CL:]
+            spot = pl.ds(pl.multiple_of(start * 8, 8) + (half + a) * 8, 8)
+            phi_ref[spot, :] = jnp.sum(s.reshape(hidden // 8, 8, CL), 0)
+            slope_ref[spot, :] = jnp.sum(g.reshape(hidden // 8, 8, CL), 0)
+
+        def step(start, used):
             rolled = pltpu.roll(proj_ref[...], lax.rem(nbasis - start + CL, CL), 1)
-            lhs = jnp.where(lanes64 < nbasis, base_ref[...], rolled)[:, : nbasis + PICK].astype(BF16)
-            for half in range(0, STEP, GROUP):
-                rows = pl.ds(pl.multiple_of(start + half, GROUP), GROUP)
-                scaled = dist_ref[rows, :]
-                for a in range(GROUP):
-                    off = scaled[a : a + 1] - centers
-                    basis = jnp.exp2(-(off * off))
-                    lift = basis * off
-                    x1 = jnp.concatenate(
-                        [jnp.concatenate([basis, lift], 1).astype(BF16), pick_ref[half + a]], 0
-                    )
-                    y1 = jnp.dot(lhs, x1, preferred_element_type=F32)
-                    h = (y1[:, :CL] + pair_ref[...]).astype(BF16)
-                    e = y1[:, CL:].astype(BF16)
-                    t = jnp.tanh(h)
-                    u = one + t
-                    s = h * u
-                    d = u + (one - t) * s
-                    x2 = jnp.concatenate([s, d * e], 1)
-                    y2 = jnp.dot(whid, x2, preferred_element_type=F32)
-                    h = y2[:, :CL]
-                    t = jnp.tanh(h)
-                    u = (1.0 + t) * wout_ref8[...]
-                    s = h * u
-                    g = (u + (1.0 - t) * s) * y2[:, CL:]
-                    spot = pl.ds(pl.multiple_of(start * 8, 8) + (half + a) * 8, 8)
-                    phi_ref[spot, :] = jnp.sum(s.reshape(hidden // 8, 8, CL), 0)
-                    slope_ref[spot, :] = jnp.sum(g.reshape(hidden // 8, 8, CL), 0)
-
-        @pl.loop(0, chunks // 2)
-        def _(c):
-            start = pl.multiple_of(c * (2 * STEP), 2 * STEP)
-            step(start)
-            step(start + STEP)
-
-        @pl.when(chunks % 2 == 1)
-        def _():
-            step(pl.multiple_of((chunks - 1) * STEP, STEP))
-
-        dist = dist_ref[...] * (spacing / scale)
-        slope = slope_ref[pl.ds(0, CL, stride=8), :]
-        phi = phi_ref[pl.ds(0, CL, stride=8), :]
-        for k in range(1, 8):
-            slope = slope + slope_ref[pl.ds(k, CL, stride=8), :]
-            phi = phi + phi_ref[pl.ds(k, CL, stride=8), :]
+            lhs = jnp.where(inside, rolled, base_ref[...])[:, :depth].astype(BF16)
+            batch = [(half, a) for half in range(0, STEP, GROUP) for a in range(used)]
+            for at in range(0, len(batch), PAIR):
+                todo = batch[at : at + PAIR]
+                hidden_in = [enter(start, used, lhs, half, a) for half, a in todo]
+                hidden_out = [jnp.dot(whid, x2, preferred_element_type=F32) for x2 in hidden_in]
+                for (half, a), y2 in zip(todo, hidden_out):
+                    leave(start, half, a, y2)
+
+        def sweep(used):
+            if used == 8:
+                pack_ref[...] = dist_ref[...]
+                pair_ref[0] = pair_src[...]
+            else:
+                pair = pair_src[...]
+                tails = [dist_ref[pl.ds(k, CL // 8, stride=8), :] for k in range(used, 8)]
+                for g in range(used):
+                    packed = dist_ref[pl.ds(g, CL // 8, stride=8), :]
+                    paired = pair
+                    for k in range(used, 8):
+                        moved = shift(tails[k - used], SEG * (k - g))
+                        packed = jnp.where(segs == k, moved, packed)
+                        paired = jnp.where(segs64 == k, shift(pair, SEG * (k - g)), paired)
+                    pack_ref[pl.ds(g, CL // 8, stride=8), :] = packed
+                    pair_ref[g] = paired
+
+            @pl.loop(0, chunks // 4)
+            def _(c):
+                start = pl.multiple_of(c * (4 * STEP), 4 * STEP)
+                for k in range(4):
+                    step(start + k * STEP, used)
+
+            done = chunks // 4 * 4
+
+            @pl.when(chunks % 4 >= 2)
+            def _():
+                start = pl.multiple_of(done * STEP, 4 * STEP)
+                step(start, used)
+                step(start + STEP, used)
+
+            @pl.when(chunks % 2 == 1)
+            def _():
+                step(pl.multiple_of((chunks - 1) * STEP, STEP), used)
+
+            for thin_ref, wide_ref in ((nphi_ref, phi_ref), (nslope_ref, slope_ref)):
+                total = wide_ref[pl.ds(0, CL, stride=8), :]
+                for k in range(1, 8):
+                    total = total + wide_ref[pl.ds(k, CL, stride=8), :]
+                thin_ref[...] = total
+                if used < 8:
+                    parts = [thin_ref[pl.ds(g, CL // 8, stride=8), :] for g in range(used)]
+                    for k in range(used, 8):
+                        tail = shift(parts[0], -SEG * k)
+                        for g in range(1, used):
+                            tail = jnp.where(segs == g, shift(parts[g], SEG * (g - k)), tail)
+                        thin_ref[pl.ds(k, CL // 8, stride=8), :] = tail
+
+        for used in WIDTHS:
+            pl.when(width == used)(functools.partial(sweep, used))
+
+        slope = nslope_ref[...]
+        phi = nphi_ref[...]
         both = jnp.logical_and(mine[:, 3:4] * right[3:4] > 0.5, same * ident < 0.5)
         weight = jnp.where(both, back * slope / dist, 0.0)
         phi = jnp.where(both, phi, 0.0)
@@ -294,13 +354,18 @@
         scratch_shapes=[
             pltpu.VMEM((ncol * cpd, CL, CL), F32),
             pltpu.VMEM((CL, CL), F32),
+            pltpu.VMEM((CL, CL), F32),
             pltpu.VMEM((CL * 8, CL), F32),
             pltpu.VMEM((CL * 8, CL), F32),
+            pltpu.VMEM((CL, CL), F32),
+            pltpu.VMEM((CL, CL), F32),
             pltpu.VMEM((hidden, CL), F32),
             pltpu.VMEM((hidden, CL), F32),
+            pltpu.VMEM((8, hidden, CL), F32),
             pltpu.VMEM((hidden, CL), F32),
             pltpu.VMEM((hidden, CL), F32),
-            pltpu.VMEM((STEP, PICK, 2 * CL), BF16),
+            pltpu.VMEM((w_radial.shape[1], CL), F32),
+            pltpu.VMEM((len(WIDTHS), STEP, PICK, 2 * CL), BF16),
         ],
     )(tiles.T, tile_count, *gathered, w_radial.T, w_hidden, w_out[None, :])
     forces, energy = pl.pallas_call(

time: 57.4 us -> 60 us (1.045); the launches traced: 56.9 us -> 60.9 us
  Pallas kernels: 53.7 us -> 57.7 us
    pallas_call x1, Pallas kernels: 13.2 us -> 31.7 us  [body(): pl.pallas_call(functools.partial(tile_kernel, cpd, ncol), name='tiles', o...]
    pallas_call x1, Pallas kernels: 25.3 us -> 10.7 us  [body(): pl.pallas_call(functools.partial(scatter_kernel, nrow, ncol), name='scatt...]
where the time goes in v1:
time: 60 us; the launch traced here: 60.9 us
  Pallas kernels  57.7 us (96%)
  local copies, waits for them, and re-layouts  1.9 us (3%)
  between operations  1.3 us (2%)
    pallas_call x1, Pallas kernels, body(): pl.pallas_call(functools.partial(tile_kernel, cpd, ncol), name='tiles', o...  31.7 us
    pallas_call x1, Pallas kernels, body(): pl.pallas_call(functools.partial(gather_kernel, nrow, ncol, inner), name=...  15.3 us
    pallas_call x1, Pallas kernels, body(): pl.pallas_call(functools.partial(scatter_kernel, nrow, ncol), name='scatt...  10.7 us
    unnamed x6, local copies, waits for them, and re-layouts  1.9 us

profile of v1, /device:TPU:0, one launch (start us, length us, event | category | flops | bytes accessed | tf_op | source)
XLA Modules:
  0.0 60.9 jit_solution(3107701033435315375)
XLA Ops:
  1.3 15.3 %gather.1 = (f32[4,4,256]{2,1,0:T(4,128)}, bf16[4,64,256]{2,1,0:T(8,128)(2,1)}, f32[8,4,256]{2,1,0:T(4,128)}, bf16[8,64,256]{2,1,0:T(8,128)(2,1)}) custom-call(f32[3,256]{1,0:T(4,128)} %pos_ref.1, bf16[128,256]{1,0:T(8,128)(2,1)} %feat_ref.1, s32[2]{0:T(128)} %fill_ref.1, bf16[64,128]{1,0:T(8,128)(2,1)} %bitcast.6, bf16[64,128]{1,0:T(8,128)(2,1)} %bitcast.7), custom_call_target="tpu_custom_call" | custom-call | tf_op jit(solution)/shard_map/gather/pallas_call | solution.py:328
  16.5 31.7 %tiles.1 = (f32[4,8,256]{2,1,0:T(8,128)}, f32[8,8,256]{2,1,0:T(8,128)}) custom-call(s32[2,8]{1,0:T(2,128)} %bitcast.9, s32[1]{0:T(128)S(6)} %copy.14.count_ref, f32[4,4,256]{2,1,0:T(4,128)} %get-tuple-element.10.rowc_ref, bf16[4,64,256]{2,1,0:T(8,128)(2,1)} %get-tuple-element.11.rowp_ref, f32[8,4,256]{2,1,0:T(4,128)} %get-tuple-element.12.colc_ref, ...), custom_call_target="tpu_custom_call" | custom-call | tf_op jit(solution)/shard_map/tiles/pallas_call | solution.py:345
  48.3 10.7 %scatter.1 = (f32[3,256]{1,0:T(4,128)}, f32[1,256]{1,0:T(1,128)}) custom-call(f32[4,8,256]{2,1,0:T(8,128)} %get-tuple-element.14.first_ref, f32[8,8,256]{2,1,0:T(8,128)} %get-tuple-element.15.second_ref), custom_call_target="tpu_custom_call" | custom-call | tf_op jit(solution)/shard_map/scatter/pallas_call | solution.py:371
  59.0 0.0 copy-start
  59.0 0.7 %copy-done = f32[3,256]{1,0:T(4,128)S(1)} copy-done((f32[3,256]{1,0:T(4,128)S(1)}, f32[3,256]{1,0:T(4,128)}, u32[]{:S(2)}) %copy-start) | copy-done | bytes 3096
  59.7 0.0 copy-start.1
  59.7 0.6 copy.15
  60.3 0.1 copy-done.1
  60.4 0.6 copy.16
Async XLA Ops:
  59.0 0.7 %copy-start = (f32[3,256]{1,0:T(4,128)S(1)}, f32[3,256]{1,0:T(4,128)}, u32[]{:S(2)}) copy-start(f32[3,256]{1,0:T(4,128)} %get-tuple-element.20) | copy-start | bytes 9220
  59.7 0.7 %copy-start.1 = (f32[1,256]{1,0:T(1,128)S(1)}, f32[1,256]{1,0:T(1,128)}, u32[]{:S(2)}) copy-start(f32[1,256]{1,0:T(1,128)} %get-tuple-element.17) | copy-start | bytes 3076

commit v2 on v1

--- a/solution.py
+++ b/solution.py
@@ -11,12 +11,11 @@
 CL = 128
 SOFT = 0.01
 RANGE = 6.0
-GROUP = 8
 STEP = 16
 PICK = 16
 SEG = 16
-PAIR = 16
-WIDTHS = (5, 6, 7, 8)
+LEAST = 4
+UNITS = 8
 MESH = pl.DeviceIdType.MESH
 F32 = jnp.float32
 BF16 = jnp.bfloat16
@@ -137,7 +136,7 @@
     cpd, ncol, tiles_ref, count_ref, rowc_ref, rowp_ref, colc_ref, colp_ref,
     wrad_ref, whid_ref, wout_ref, first_ref, second_ref,
     acc_ref, dist_ref, pack_ref, phi_ref, slope_ref, nphi_ref, nslope_ref,
-    proj_ref, pair_src, pair_ref, base_ref, wout_ref8, cent_ref, pick_ref,
+    proj_ref, pair_src, pair_ref, base_ref, wout_ref8, cent_ref, lhs_ref, pick_ref,
 ):
     row = lax.axis_index("row")
     col = lax.axis_index("col")
@@ -167,14 +166,9 @@
     segs = lax.broadcasted_iota(jnp.int32, (CL // 8, CL), 1) // SEG
     lanes = lax.broadcasted_iota(jnp.int32, (CL, CL), 1)
     ident = (lax.broadcasted_iota(jnp.int32, (CL, CL), 0) == lanes).astype(F32)
-    pick = lax.broadcasted_iota(jnp.int32, (PICK, 2 * CL), 0)
-    pick_lane = lax.broadcasted_iota(jnp.int32, (PICK, 2 * CL), 1)
-    for used in WIDTHS:
-        for a in range(STEP):
-            if a % 8 < used:
-                source = jnp.where(pick_lane < used * SEG, a % 8, pick_lane // SEG) + a // 8 * 8
-                hit = jnp.logical_and(pick == source, pick_lane < CL)
-                pick_ref[used - WIDTHS[0], a] = jnp.where(hit, 1.0, 0.0).astype(BF16)
+    pick = lax.broadcasted_iota(jnp.int32, (PICK, CL), 0)
+    pick_seg = lax.broadcasted_iota(jnp.int32, (PICK, CL), 1) // SEG
+    pick_ref[...] = jnp.zeros_like(pick_ref)
 
     def shift(value, amount):
         amount = amount % CL
@@ -199,99 +193,98 @@
         beads = jnp.sum(left[3:4]).astype(jnp.int32)
         chunks = (beads + STEP - 1) // STEP
         across = jnp.sum(right[3:4]).astype(jnp.int32)
-        width = jnp.maximum((across + SEG - 1) // SEG, WIDTHS[0])
+        width = jnp.maximum((across + SEG - 1) // SEG, LEAST)
         dx = mine[:, 0:1] - right[0:1]
         dy = mine[:, 1:2] - right[1:2]
         dz = mine[:, 2:3] - right[2:3]
         dist = jnp.sqrt(dx * dx + dy * dy + dz * dz + SOFT)
         dist_ref[...] = dist * (scale / spacing)
 
-        def enter(start, used, lhs, half, a):
-            scaled = pack_ref[pl.ds(start + (half + a), 1), :]
-            off = scaled - cent_ref[...]
+        for g in range(8):
+            source = jnp.where(pick_seg < width, g, pick_seg)
+            for p in range(2):
+                pick_ref[2 * g + p, :, :CL] = jnp.where(pick == source + 8 * p, 1.0, 0.0).astype(BF16)
+        for c in range(CL // STEP):
+            rolled = shift(proj_ref[...], nbasis - STEP * c)
+            lhs_ref[c] = jnp.where(inside, rolled, base_ref[...]).astype(BF16)
+        spare = segs >= width
+        spare64 = segs64 >= width
+        tails = [dist_ref[pl.ds(k, CL // 8, stride=8), :] for k in range(LEAST, 8)]
+        for g in range(8):
+            moved = shift(tails[0], SEG * (LEAST - g))
+            for k in range(LEAST + 1, 8):
+                moved = jnp.where(segs >= k, shift(tails[k - LEAST], SEG * (k - g)), moved)
+            packed = dist_ref[pl.ds(g, CL // 8, stride=8), :]
+            pack_ref[pl.ds(g, CL // 8, stride=8), :] = jnp.where(spare, moved, packed)
+        for at in range(0, hidden, 8):
+            part = pair_src[at : at + 8, :]
+            turned = {j: shift(part, SEG * j) for j in range(LEAST - 7, 8)}
+            for g in range(8):
+                moved = turned[LEAST - g]
+                for k in range(LEAST + 1, 8):
+                    moved = jnp.where(segs[:8] >= k, turned[k - g], moved)
+                pair_ref[g, at : at + 8, :] = jnp.where(spare64[:8], moved, part)
+
+        def enter(c, g, p):
+            off = pack_ref[pl.ds(c * STEP + p * 8 + g, 1), :] - cent_ref[...]
             basis = jnp.exp2(-(off * off))
             lift = basis * off
             bump = jnp.concatenate([basis, lift], 1).astype(BF16)
-            x1 = jnp.concatenate([bump, pick_ref[used - WIDTHS[0], half + a], bump], 0)
-            y1 = jnp.dot(lhs, x1, preferred_element_type=F32)
-            h = y1[:, :CL] + pair_ref[a if used < 8 else 0]
+            x1 = jnp.concatenate([bump, pick_ref[2 * g + p], bump], 0)
+            y1 = jnp.dot(lhs_ref[c, :, :depth], x1, preferred_element_type=F32)
+            h = y1[:, :CL] + pair_ref[g]
             t = jnp.tanh(h)
             u = 1.0 + t
             s = h * u
             d = (u + (1.0 - t) * s) * y1[:, CL:]
             return jnp.concatenate([s, d], 1).astype(BF16)
 
-        def leave(start, half, a, y2):
+        def leave(c, g, p, y2):
             h = y2[:, :CL]
             t = jnp.tanh(h)
             u = (1.0 + t) * wout_ref8[...]
             s = h * u
-            g = (u + (1.0 - t) * s) * y2[:, CL:]
-            spot = pl.ds(pl.multiple_of(start * 8, 8) + (half + a) * 8, 8)
+            d = (u + (1.0 - t) * s) * y2[:, CL:]
+            spot = pl.ds(pl.multiple_of((c * STEP + p * 8 + g) * 8, 8), 8)
             phi_ref[spot, :] = jnp.sum(s.reshape(hidden // 8, 8, CL), 0)
-            slope_ref[spot, :] = jnp.sum(g.reshape(hidden // 8, 8, CL), 0)
-
-        def step(start, used):
-            rolled = pltpu.roll(proj_ref[...], lax.rem(nbasis - start + CL, CL), 1)
-            lhs = jnp.where(inside, rolled, base_ref[...])[:, :depth].astype(BF16)
-            batch = [(half, a) for half in range(0, STEP, GROUP) for a in range(used)]
-            for at in range(0, len(batch), PAIR):
-                todo = batch[at : at + PAIR]
-                hidden_in = [enter(start, used, lhs, half, a) for half, a in todo]
-                hidden_out = [jnp.dot(whid, x2, preferred_element_type=F32) for x2 in hidden_in]
-                for (half, a), y2 in zip(todo, hidden_out):
-                    leave(start, half, a, y2)
-
-        def sweep(used):
-            if used == 8:
-                pack_ref[...] = dist_ref[...]
-                pair_ref[0] = pair_src[...]
-            else:
-                pair = pair_src[...]
-                tails = [dist_ref[pl.ds(k, CL // 8, stride=8), :] for k in range(used, 8)]
-                for g in range(used):
-                    packed = dist_ref[pl.ds(g, CL // 8, stride=8), :]
-                    paired = pair
-                    for k in range(used, 8):
-                        moved = shift(tails[k - used], SEG * (k - g))
-                        packed = jnp.where(segs == k, moved, packed)
-                        paired = jnp.where(segs64 == k, shift(pair, SEG * (k - g)), paired)
-                    pack_ref[pl.ds(g, CL // 8, stride=8), :] = packed
-                    pair_ref[g] = paired
-
-            @pl.loop(0, chunks // 4)
-            def _(c):
-                start = pl.multiple_of(c * (4 * STEP), 4 * STEP)
-                for k in range(4):
-                    step(start + k * STEP, used)
-
-            done = chunks // 4 * 4
-
-            @pl.when(chunks % 4 >= 2)
-            def _():
-                start = pl.multiple_of(done * STEP, 4 * STEP)
-                step(start, used)
-                step(start + STEP, used)
-
-            @pl.when(chunks % 2 == 1)
-            def _():
-                step(pl.multiple_of((chunks - 1) * STEP, STEP), used)
-
-            for thin_ref, wide_ref in ((nphi_ref, phi_ref), (nslope_ref, slope_ref)):
-                total = wide_ref[pl.ds(0, CL, stride=8), :]
-                for k in range(1, 8):
-                    total = total + wide_ref[pl.ds(k, CL, stride=8), :]
-                thin_ref[...] = total
-                if used < 8:
-                    parts = [thin_ref[pl.ds(g, CL // 8, stride=8), :] for g in range(used)]
-                    for k in range(used, 8):
-                        tail = shift(parts[0], -SEG * k)
-                        for g in range(1, used):
-                            tail = jnp.where(segs == g, shift(parts[g], SEG * (g - k)), tail)
-                        thin_ref[pl.ds(k, CL // 8, stride=8), :] = tail
-
-        for used in WIDTHS:
-            pl.when(width == used)(functools.partial(sweep, used))
+            slope_ref[spot, :] = jnp.sum(d.reshape(hidden // 8, 8, CL), 0)
+
+        def block(units, place):
+            c, g = place
+            for at in range(0, units, UNITS):
+                todo = []
+                for _ in range(min(UNITS, units)):
+                    for p in range(2):
+                        todo.append((jnp.minimum(c, CL // STEP - 1), g, p))
+                    wrap = g + 1 == width
+                    c = c + jnp.where(wrap, 1, 0)
+                    g = jnp.where(wrap, 0, g + 1)
+                inner = [enter(*row) for row in todo]
+                outer = [jnp.dot(whid, x2, preferred_element_type=F32) for x2 in inner]
+                for row, y2 in zip(todo, outer):
+                    leave(*row, y2)
+            return c, g
+
+        count = chunks * width
+        large = (count + UNITS - 1) // (2 * UNITS)
+        origin = (jnp.int32(0), jnp.int32(0))
+        place = lax.fori_loop(0, large, lambda _, at: block(2 * UNITS, at), origin)
+
+        @pl.when(count > large * 2 * UNITS)
+        def _():
+            block(UNITS, place)
+
+        for thin_ref, wide_ref in ((nphi_ref, phi_ref), (nslope_ref, slope_ref)):
+            total = wide_ref[pl.ds(0, CL, stride=8), :]
+            for k in range(1, 8):
+                total = total + wide_ref[pl.ds(k, CL, stride=8), :]
+            thin_ref[...] = total
+            parts = [thin_ref[pl.ds(g, CL // 8, stride=8), :] for g in range(8)]
+            for k in range(LEAST, 8):
+                tail = shift(parts[0], -SEG * k)
+                for g in range(1, 7):
+                    tail = jnp.where(segs == g, shift(parts[g], SEG * (g - k)), tail)
+                thin_ref[pl.ds(k, CL // 8, stride=8), :] = jnp.where(width > k, parts[k], tail)
 
         slope = nslope_ref[...]
         phi = nphi_ref[...]
@@ -365,7 +358,8 @@
             pltpu.VMEM((hidden, CL), F32),
             pltpu.VMEM((hidden, CL), F32),
             pltpu.VMEM((w_radial.shape[1], CL), F32),
-            pltpu.VMEM((len(WIDTHS), STEP, PICK, 2 * CL), BF16),
+            pltpu.VMEM((CL // STEP, hidden, CL), BF16),
+            pltpu.VMEM((16, PICK, 2 * CL), BF16),
         ],
     )(tiles.T, tile_count, *gathered, w_radial.T, w_hidden, w_out[None, :])
     forces, energy = pl.pallas_call(

time: 60 us -> 57.2 us (0.953); the launches traced: 60.9 us -> 56.9 us
  Pallas kernels: 57.7 us -> 53.7 us
    pallas_call x1, Pallas kernels: 31.7 us -> 26.2 us  [body(): pl.pallas_call(functools.partial(tile_kernel, cpd, ncol), name='tiles', o...]
    pallas_call x1, Pallas kernels: 10.7 us -> 12.2 us  [body(): pl.pallas_call(functools.partial(scatter_kernel, nrow, ncol), name='scatt...]
where the time goes in v2:
time: 57.2 us; the launch traced here: 56.9 us
  Pallas kernels  53.7 us (94%)
  local copies, waits for them, and re-layouts  1.9 us (3%)
  between operations  1.3 us (2%)
    pallas_call x1, Pallas kernels, body(): pl.pallas_call(functools.partial(tile_kernel, cpd, ncol), name='tiles', o...  26.2 us
    pallas_call x1, Pallas kernels, body(): pl.pallas_call(functools.partial(gather_kernel, nrow, ncol, inner), name=...  15.3 us
    pallas_call x1, Pallas kernels, body(): pl.pallas_call(functools.partial(scatter_kernel, nrow, ncol), name='scatt...  12.2 us
    unnamed x6, local copies, waits for them, and re-layouts  1.9 us

profile of v2, /device:TPU:0, one launch (start us, length us, event | category | flops | bytes accessed | tf_op | source)
XLA Modules:
  0.0 56.9 jit_solution(4106949898984305368)
XLA Ops:
  1.3 15.3 %gather.1 = (f32[4,4,256]{2,1,0:T(4,128)}, bf16[4,64,256]{2,1,0:T(8,128)(2,1)}, f32[8,4,256]{2,1,0:T(4,128)}, bf16[8,64,256]{2,1,0:T(8,128)(2,1)}) custom-call(f32[3,256]{1,0:T(4,128)} %pos_ref.1, bf16[128,256]{1,0:T(8,128)(2,1)} %feat_ref.1, s32[2]{0:T(128)} %fill_ref.1, bf16[64,128]{1,0:T(8,128)(2,1)} %bitcast.6, bf16[64,128]{1,0:T(8,128)(2,1)} %bitcast.7), custom_call_target="tpu_custom_call" | custom-call | tf_op jit(solution)/shard_map/gather/pallas_call | solution.py:321
  16.5 26.2 %tiles.1 = (f32[4,8,256]{2,1,0:T(8,128)}, f32[8,8,256]{2,1,0:T(8,128)}) custom-call(s32[2,8]{1,0:T(2,128)} %bitcast.9, s32[1]{0:T(128)S(6)} %copy.14.count_ref, f32[4,4,256]{2,1,0:T(4,128)} %get-tuple-element.10.rowc_ref, bf16[4,64,256]{2,1,0:T(8,128)(2,1)} %get-tuple-element.11.rowp_ref, f32[8,4,256]{2,1,0:T(4,128)} %get-tuple-element.12.colc_ref, ...), custom_call_target="tpu_custom_call" | custom-call | tf_op jit(solution)/shard_map/tiles/pallas_call | solution.py:338
  42.7 12.2 %scatter.1 = (f32[3,256]{1,0:T(4,128)}, f32[1,256]{1,0:T(1,128)}) custom-call(f32[4,8,256]{2,1,0:T(8,128)} %get-tuple-element.14.first_ref, f32[8,8,256]{2,1,0:T(8,128)} %get-tuple-element.15.second_ref), custom_call_target="tpu_custom_call" | custom-call | tf_op jit(solution)/shard_map/scatter/pallas_call | solution.py:365
  55.0 0.0 copy-start
  55.0 0.7 %copy-done = f32[3,256]{1,0:T(4,128)S(1)} copy-done((f32[3,256]{1,0:T(4,128)S(1)}, f32[3,256]{1,0:T(4,128)}, u32[]{:S(2)}) %copy-start) | copy-done | bytes 3096
  55.6 0.0 copy-start.1
  55.6 0.6 %copy.15 = f32[3,256]{1,0:T(4,128)} copy(f32[3,256]{1,0:T(4,128)S(1)} %copy-done) | data formatting | bytes 6144
  56.2 0.1 copy-done.1
  56.3 0.6 copy.16
Async XLA Ops:
  55.0 0.7 %copy-start = (f32[3,256]{1,0:T(4,128)S(1)}, f32[3,256]{1,0:T(4,128)}, u32[]{:S(2)}) copy-start(f32[3,256]{1,0:T(4,128)} %get-tuple-element.20) | copy-start | bytes 9220
  55.6 0.7 %copy-start.1 = (f32[1,256]{1,0:T(1,128)S(1)}, f32[1,256]{1,0:T(1,128)}, u32[]{:S(2)}) copy-start(f32[1,256]{1,0:T(1,128)} %get-tuple-element.17) | copy-start | bytes 3076

commit v3 on v2

--- a/solution.py
+++ b/solution.py
@@ -100,7 +100,7 @@
 
 
 def scatter_kernel(
-    nrow, ncol, first_ref, second_ref, force_ref, energy_ref, row_in, col_in, send_sem, recv_sem
+    nrow, ncol, first_ref, second_ref, total_ref, other_ref, row_in, col_in, send_sem, recv_sem
 ):
     i = lax.axis_index("row")
     j = lax.axis_index("col")
@@ -128,8 +128,8 @@
         total = total + row_in[d]
     for d in range(1, nrow):
         other = other + col_in[d]
-    force_ref[...] = total[:3] + other[:3]
-    energy_ref[...] = total[3:4]
+    total_ref[...] = total[:4]
+    other_ref[...] = other[:3]
 
 
 def tile_kernel(
@@ -362,12 +362,12 @@
             pltpu.VMEM((16, PICK, 2 * CL), BF16),
         ],
     )(tiles.T, tile_count, *gathered, w_radial.T, w_hidden, w_out[None, :])
-    forces, energy = pl.pallas_call(
+    total, other = pl.pallas_call(
         functools.partial(scatter_kernel, nrow, ncol),
         name="scatter",
         out_shape=(
+            jax.ShapeDtypeStruct((4, beads), F32),
             jax.ShapeDtypeStruct((3, beads), F32),
-            jax.ShapeDtypeStruct((1, beads), F32),
         ),
         in_specs=[vmem, vmem],
         out_specs=(vmem, vmem),
@@ -379,7 +379,7 @@
         ],
         compiler_params=pltpu.CompilerParams(collective_id=1, has_side_effects=True),
     )(firsts, seconds)
-    return forces, energy[0]
+    return total[:3] + other, total[3]
 
 
 def solution(mesh):

time: 57.2 us -> 61.1 us (1.068)
  Pallas kernels: 53.7 us -> 57.1 us
  other arithmetic: 0 us -> 1.28 us
  local copies, waits for them, and re-layouts: 1.9 us -> 1.24 us
    pallas_call x1, Pallas kernels: 12.2 us -> 31.4 us  [body(): pl.pallas_call(functools.partial(scatter_kernel, nrow, ncol), name='scatt...]
    pallas_call x1, Pallas kernels: 26.2 us -> 10.4 us  [body(): pl.pallas_call(functools.partial(tile_kernel, cpd, ncol), name='tiles', o...]
    unnamed x6 -> x0, local copies, waits for them, and re-layouts: 1.9 us -> none
    add x0 -> x1, other arithmetic: none -> 1.28 us  [body(): return (total[:3] + other, total[3])]
    slice x0 -> x1, local copies, waits for them, and re-layouts: none -> 1.24 us  [body(): return (total[:3] + other, total[3])]
where the time goes in v3:
time: 61.1 us; the launch traced here: 60.9 us
  Pallas kernels  57.1 us (93%)
  between operations  1.29 us (2%)
  other arithmetic  1.28 us (2%)
  local copies, waits for them, and re-layouts  1.24 us (2%)
    pallas_call x1, Pallas kernels, body(): pl.pallas_call(functools.partial(scatter_kernel, nrow, ncol), name='scatt...  31.4 us
    pallas_call x1, Pallas kernels, body(): pl.pallas_call(functools.partial(gather_kernel, nrow, ncol, inner), name=...  15.3 us
    pallas_call x1, Pallas kernels, body(): pl.pallas_call(functools.partial(tile_kernel, cpd, ncol), name='tiles', o...  10.4 us
    add x1, other arithmetic, body(): return (total[:3] + other, total[3])  1.28 us
    slice x1, local copies, waits for them, and re-layouts, body(): return (total[:3] + other, total[3])  1.24 us

profile of v3, /device:TPU:0, one launch (start us, length us, event | category | flops | bytes accessed | tf_op | source)
XLA Modules:
  0.0 60.9 jit_solution(6275779873640498019)
XLA Ops:
  1.3 15.3 %gather.1 = (f32[4,4,256]{2,1,0:T(4,128)}, bf16[4,64,256]{2,1,0:T(8,128)(2,1)}, f32[8,4,256]{2,1,0:T(4,128)}, bf16[8,64,256]{2,1,0:T(8,128)(2,1)}) custom-call(f32[3,256]{1,0:T(4,128)} %pos_ref.1, bf16[128,256]{1,0:T(8,128)(2,1)} %feat_ref.1, s32[2]{0:T(128)} %fill_ref.1, bf16[64,128]{1,0:T(8,128)(2,1)} %bitcast.6, bf16[64,128]{1,0:T(8,128)(2,1)} %bitcast.7), custom_call_target="tpu_custom_call" | custom-call | tf_op jit(solution)/shard_map/gather/pallas_call | solution.py:321
  16.5 10.4 %tiles.1 = (f32[4,8,256]{2,1,0:T(8,128)}, f32[8,8,256]{2,1,0:T(8,128)}) custom-call(s32[2,8]{1,0:T(2,128)} %bitcast.9, s32[1]{0:T(128)S(6)} %copy.12.count_ref, f32[4,4,256]{2,1,0:T(4,128)} %get-tuple-element.10.rowc_ref, bf16[4,64,256]{2,1,0:T(8,128)(2,1)} %get-tuple-element.11.rowp_ref, f32[8,4,256]{2,1,0:T(4,128)} %get-tuple-element.12.colc_ref, ...), custom_call_target="tpu_custom_call" | custom-call | tf_op jit(solution)/shard_map/tiles/pallas_call | solution.py:338
  27.0 31.4 %scatter.1 = (f32[4,256]{1,0:T(4,128)}, f32[3,256]{1,0:T(4,128)}) custom-call(f32[4,8,256]{2,1,0:T(8,128)} %get-tuple-element.14.first_ref, f32[8,8,256]{2,1,0:T(8,128)} %get-tuple-element.15.second_ref), custom_call_target="tpu_custom_call" | custom-call | tf_op jit(solution)/shard_map/scatter/pallas_call | solution.py:365
  58.3 1.3 %slice_add_fusion = f32[3,256]{1,0:T(4,128)} fusion(f32[3,256]{1,0:T(4,128)} %get-tuple-element.17, f32[4,256]{1,0:T(4,128)} %get-tuple-element.16), kind=kLoop, calls=%fused_computation | loop fusion | flops 768 | bytes 9216 | tf_op jit(solution)/shard_map/add | solution.py:382
  59.6 1.2 %slice.7 = f32[1,256]{1,0:T(1,128)} slice(f32[4,256]{1,0:T(4,128)} %get-tuple-element.16), slice={[3:4], [0:256]} | slice | bytes 2048 | tf_op jit(solution)/shard_map/slice | solution.py:382
